TPU v7x, 32 devices: a whole 2x2x4 slice. The times are simulated.
32 devices in a mesh: wide: 16 (over z, y, x), narrow: 2 (over core).
Axes of the slice: x: 2, y: 2, z: 4, core: 2. Of those that a mesh axis runs over, the one named last changes fastest.
Arguments:
- tokens: bfloat16 [16384, 1024], P(('wide', 'narrow')), may hold values from -6 to 6
- window_span: int32 [32], P('wide'), may hold values from 1 to 2, as said below
- valid_len: int32 [32], P('wide'), may hold values from 384 to 512, as said below
- norm1_gain: float32 [1024], replicated, may hold values from 0.5 to 1.5
- norm1_shift: float32 [1024], replicated, may hold values from -1.8 to 1.8
- w_query: bfloat16 [1024, 1024], P(None, 'narrow'), may hold values from -0.25 to 0.25
- w_key: bfloat16 [1024, 1024], P(None, 'narrow'), may hold values from -0.25 to 0.25
- w_value: bfloat16 [1024, 1024], P(None, 'narrow'), may hold values from -0.1875 to 0.1875
- w_out: bfloat16 [1024, 1024], P('narrow'), may hold values from -1.5 to 1.5
- norm2_gain: float32 [1024], replicated, may hold values from 0.5 to 1.5
- norm2_shift: float32 [1024], replicated, may hold values from -1.8 to 1.8
- w_gate: bfloat16 [1024, 4096], P(None, 'narrow'), may hold values from -0.1875 to 0.1875
- w_up: bfloat16 [1024, 4096], P(None, 'narrow'), may hold values from -0.1875 to 0.1875
- w_down: bfloat16 [4096, 1024], P('narrow'), may hold values from -0.09375 to 0.09375
- cotangent: bfloat16 [16384, 1024], P(('wide', 'narrow')), may hold values from -6 to 6
Outputs:
- out: float32 [16384, 1024], P(('wide', 'narrow'))
- token_grad: float32 [16384, 1024], P(('wide', 'narrow'))
- norm1_gain_grad: float32 [1024], replicated
- norm1_shift_grad: float32 [1024], replicated
- w_query_grad: float32 [1024, 1024], P(None, 'narrow')
- w_key_grad: float32 [1024, 1024], P(None, 'narrow')
- w_value_grad: float32 [1024, 1024], P(None, 'narrow')
- w_out_grad: float32 [1024, 1024], P('narrow')
- norm2_gain_grad: float32 [1024], replicated
- norm2_shift_grad: float32 [1024], replicated
- w_gate_grad: float32 [1024, 4096], P(None, 'narrow')
- w_up_grad: float32 [1024, 4096], P(None, 'narrow')
- w_down_grad: float32 [4096, 1024], P('narrow')
Inputs may be any that keep to these rules, and one draw needn't show every extreme that they name: `window_span`: within each group, blocks 2k and 2k+1 hold the same value: 2 where one window fills both blocks, 1 where each block holds a window of its own. `valid_len`: blocks whose window_span is 2 hold 512.
All inputs are finite; a program needn't handle non-finite values.
Results may differ from a plain program's by a relative error of at most 0.019.
Values may be sent and summed in bfloat16 or wider, within the bound.
A program may use at most 256 MiB of HBM per device.

v0:
```python
import jax
import jax.numpy as jnp
from jax import lax
from jax.sharding import PartitionSpec as P

HD = 64
EPSILON = 1e-05
MASKED = -1e30
ROPE_BASE = 10000.0


def times_transpose(left, right):
    return lax.dot_general(
        left, right, (((1,), (1,)), ((), ())), preferred_element_type=jnp.float32
    )


def transpose_times(left, right):
    return lax.dot_general(
        left, right, (((0,), (0,)), ((), ())), preferred_element_type=jnp.float32
    )


def norm_forward(values, norm_gain, norm_shift):
    average = jnp.mean(values, axis=-1, keepdims=True)
    centred = values - average
    inverse = lax.rsqrt(jnp.mean(centred * centred, axis=-1, keepdims=True) + EPSILON)
    scaled = centred * inverse
    return (scaled * norm_gain + norm_shift, scaled, inverse)


def norm_backward(grad_out, scaled, inverse, norm_gain):
    grad_scaled = grad_out * norm_gain
    first_term = jnp.mean(grad_scaled, axis=-1, keepdims=True)
    second_term = jnp.mean(grad_scaled * scaled, axis=-1, keepdims=True)
    grad_in = inverse * (grad_scaled - first_term - scaled * second_term)
    return (grad_in, jnp.sum(grad_out * scaled, axis=0), jnp.sum(grad_out, axis=0))


def rotary_tables(span_table, block_rows, width):
    row_count = span_table.shape[0] * block_rows
    row_ids = jnp.arange(row_count)
    block_ids = row_ids // block_rows
    span_rows = jnp.repeat(span_table, block_rows)
    position = (row_ids % block_rows + block_rows * (block_ids % 2) * (span_rows == 2)).astype(
        jnp.float32
    )
    columns = jnp.arange(width) % HD
    half_dim = HD // 2
    freq_index = (columns % half_dim).astype(jnp.float32)
    frequency = ROPE_BASE ** (-2.0 * freq_index / HD)
    angles = position[:, None] * frequency[None, :]
    signs = jnp.where(columns < half_dim, -1.0, 1.0).astype(jnp.float32)
    return (jnp.cos(angles), jnp.sin(angles) * signs)


def swap_halves(values):
    row_count = values.shape[0]
    width = values.shape[1]
    parts = values.reshape(row_count, width // HD, 2, HD // 2)
    return jnp.flip(parts, axis=2).reshape(row_count, width)


def rotate(values, cosine, sine_signed):
    return values * cosine + swap_halves(values) * sine_signed


def rotate_back(grads_in, cosine, sine_signed):
    return grads_in * cosine + swap_halves(grads_in * sine_signed)


def pair_mask(block_index, span_table, valid_table, block_rows):
    pair_first = block_index // 2 * 2
    offsets = jnp.arange(2 * block_rows)
    key_block = pair_first + offsets // block_rows
    within = offsets % block_rows
    first_len = lax.dynamic_index_in_dim(valid_table, pair_first, keepdims=False)
    second_len = lax.dynamic_index_in_dim(valid_table, pair_first + 1, keepdims=False)
    own_span = lax.dynamic_index_in_dim(span_table, block_index, keepdims=False)
    length_bound = jnp.where(offsets < block_rows, first_len, second_len)
    return (within < length_bound) & ((own_span == 2) | (key_block == block_index))


def on_device(
    tokens,
    window_span,
    valid_len,
    norm1_gain,
    norm1_shift,
    w_query,
    w_key,
    w_value,
    w_out,
    norm2_gain,
    norm2_shift,
    w_gate,
    w_up,
    w_down,
    cotangent,
):
    local_rows = tokens.shape[0]
    group_rows = local_rows * lax.axis_size("narrow")
    block_count = window_span.shape[0]
    block_rows = group_rows // block_count
    local_width = w_query.shape[1]
    local_heads = local_width // HD
    local_hidden = w_gate.shape[1]
    softmax_scale = HD ** (-0.5)
    token_values = tokens.astype(jnp.float32)
    normed_one, scaled_one, inverse_one = norm_forward(token_values, norm1_gain, norm1_shift)
    normed_one = normed_one.astype(jnp.bfloat16)
    gathered_one = lax.all_gather(normed_one, "narrow", axis=0, tiled=True)
    joined_qkv = jnp.concatenate([w_query, w_key, w_value], axis=1)
    projected = jnp.dot(gathered_one, joined_qkv, preferred_element_type=jnp.float32)
    cosine, sine_signed = rotary_tables(window_span, block_rows, local_width)
    query_rows = (rotate(projected[:, :local_width], cosine, sine_signed) * softmax_scale).astype(
        jnp.bfloat16
    )
    key_rows = rotate(projected[:, local_width : 2 * local_width], cosine, sine_signed).astype(
        jnp.bfloat16
    )
    value_rows = projected[:, 2 * local_width :].astype(jnp.bfloat16)

    def block_slices(block_index):
        query_block = lax.dynamic_slice_in_dim(query_rows, block_index * block_rows, block_rows, 0)
        pair_start = block_index // 2 * 2 * block_rows
        return (
            query_block.reshape(block_rows, local_heads, HD),
            key_rows.reshape(2 * block_rows, local_heads, HD),
            value_rows.reshape(2 * block_rows, local_heads, HD),
            pair_start,
        )

    def masked_scores(block_index, query_block, key_pair):
        scores = jnp.einsum(
            "qhd,khd->hqk", query_block, key_pair, preferred_element_type=jnp.float32
        )
        key_mask = pair_mask(block_index, window_span, valid_len, block_rows)
        return jnp.where(key_mask[None, None, :], scores, MASKED)

    def attend_forward(block_index):
        query_block, key_pair, value_pair, pair_start = block_slices(block_index)
        scores = masked_scores(block_index, query_block, key_pair)
        highest = jnp.max(scores, axis=-1, keepdims=True)
        weights = jnp.exp(scores - highest)
        weight_total = jnp.sum(weights, axis=-1, keepdims=True)
        attention_probs = (weights / weight_total).astype(jnp.bfloat16)
        mixed_block = jnp.einsum(
            "hqk,khd->qhd", attention_probs, value_pair, preferred_element_type=jnp.float32
        )
        return (
            mixed_block.reshape(block_rows, local_width).astype(jnp.bfloat16),
            (highest + jnp.log(weight_total))[:, :, 0],
        )

    mixed_blocks, log_totals = lax.map(attend_forward, jnp.arange(block_count))
    mixed_rows = mixed_blocks.reshape(group_rows, local_width)
    resid_values = token_values + lax.psum_scatter(
        jnp.dot(mixed_rows, w_out, preferred_element_type=jnp.float32),
        "narrow",
        scatter_dimension=0,
        tiled=True,
    )
    normed_two, scaled_two, inverse_two = norm_forward(resid_values, norm2_gain, norm2_shift)
    normed_two = normed_two.astype(jnp.bfloat16)
    gathered_two = lax.all_gather(normed_two, "narrow", axis=0, tiled=True)
    joined_gate_up = jnp.concatenate([w_gate, w_up], axis=1)
    gate_up = jnp.dot(gathered_two, joined_gate_up, preferred_element_type=jnp.float32)
    gate_values = gate_up[:, :local_hidden]
    up_values = gate_up[:, local_hidden:]
    sigmoid_gate = jax.nn.sigmoid(gate_values)
    hidden_rows = (gate_values * sigmoid_gate * up_values).astype(jnp.bfloat16)
    out_values = resid_values + lax.psum_scatter(
        jnp.dot(hidden_rows, w_down, preferred_element_type=jnp.float32).astype(jnp.bfloat16),
        "narrow",
        scatter_dimension=0,
        tiled=True,
    ).astype(jnp.float32)
    shard_rows = lax.all_gather(cotangent, "narrow", axis=0, tiled=True)
    grad_hidden = times_transpose(shard_rows, w_down)
    grad_down_w, grad_hidden = (transpose_times(hidden_rows, shard_rows), grad_hidden)
    silu_grad = sigmoid_gate * (1.0 + gate_values * (1.0 - sigmoid_gate))
    grad_gate_up = jnp.concatenate(
        [grad_hidden * up_values * silu_grad, grad_hidden * gate_values * sigmoid_gate], axis=1
    ).astype(jnp.bfloat16)
    grad_normed_two = lax.psum_scatter(
        times_transpose(grad_gate_up, joined_gate_up), "narrow", scatter_dimension=0, tiled=True
    )
    grad_gate_up_w = transpose_times(gathered_two, grad_gate_up)
    grad_in_two, gain_two_grad, shift_two_grad = norm_backward(
        grad_normed_two, scaled_two, inverse_two, norm2_gain
    )
    grad_resid = cotangent.astype(jnp.float32) + grad_in_two
    shard_rows = lax.all_gather(grad_resid.astype(jnp.bfloat16), "narrow", axis=0, tiled=True)
    grad_mixed_sum = times_transpose(shard_rows, w_out)
    grad_out_w, grad_mixed_sum = (transpose_times(mixed_rows, shard_rows), grad_mixed_sum)
    grad_mixed = grad_mixed_sum.astype(jnp.bfloat16)

    def attend_backward(block_index, running):
        grad_query, grad_key, grad_value = running
        query_block, key_pair, value_pair, pair_start = block_slices(block_index)
        grad_rows = lax.dynamic_slice_in_dim(
            grad_mixed, block_index * block_rows, block_rows, 0
        ).reshape(block_rows, local_heads, HD)
        scores = masked_scores(block_index, query_block, key_pair)
        log_total = lax.dynamic_index_in_dim(log_totals, block_index, keepdims=False)
        attention_probs = jnp.exp(scores - log_total[:, :, None])
        grad_probs = jnp.einsum(
            "qhd,khd->hqk", grad_rows, value_pair, preferred_element_type=jnp.float32
        )
        centre = jnp.sum(attention_probs * grad_probs, axis=-1, keepdims=True)
        grad_scores = (attention_probs * (grad_probs - centre)).astype(jnp.bfloat16)
        block_query = jnp.einsum(
            "hqk,khd->qhd", grad_scores, key_pair, preferred_element_type=jnp.float32
        ).reshape(block_rows, local_width)
        pair_key = jnp.einsum(
            "hqk,qhd->khd", grad_scores, query_block, preferred_element_type=jnp.float32
        ).reshape(2 * block_rows, local_width)
        pair_value = jnp.einsum(
            "hqk,qhd->khd",
            attention_probs.astype(jnp.bfloat16),
            grad_rows,
            preferred_element_type=jnp.float32,
        ).reshape(2 * block_rows, local_width)
        grad_query = lax.dynamic_update_slice_in_dim(
            grad_query, block_query, block_index * block_rows, 0
        )
        grad_key = grad_key + pair_key
        grad_value = grad_value + pair_value
        return (grad_query, grad_key, grad_value)

    zero_rows = jnp.zeros((group_rows, local_width), jnp.float32)
    grad_query, grad_key, grad_value = lax.fori_loop(
        0, block_count, attend_backward, (zero_rows, zero_rows, zero_rows)
    )
    grad_query_raw = rotate_back(grad_query * softmax_scale, cosine, sine_signed)
    grad_key_raw = rotate_back(grad_key, cosine, sine_signed)
    grad_qkv = jnp.concatenate([grad_query_raw, grad_key_raw, grad_value], axis=1).astype(
        jnp.bfloat16
    )
    grad_normed_one = lax.psum_scatter(
        times_transpose(grad_qkv, joined_qkv).astype(jnp.bfloat16),
        "narrow",
        scatter_dimension=0,
        tiled=True,
    ).astype(jnp.float32)
    grad_qkv_w = transpose_times(gathered_one, grad_qkv)
    grad_in_one, gain_one_grad, shift_one_grad = norm_backward(
        grad_normed_one, scaled_one, inverse_one, norm1_gain
    )
    token_grad = grad_resid + grad_in_one
    qkv_summed, out_summed, gate_up_summed, down_summed = (
        lax.psum(grad_qkv_w.astype(jnp.bfloat16), "wide").astype(jnp.float32),
        lax.psum(grad_out_w.astype(jnp.bfloat16), "wide").astype(jnp.float32),
        lax.psum(grad_gate_up_w.astype(jnp.bfloat16), "wide").astype(jnp.float32),
        lax.psum(grad_down_w.astype(jnp.bfloat16), "wide").astype(jnp.float32),
    )
    norm_summed = lax.psum(
        (gain_one_grad, shift_one_grad, gain_two_grad, shift_two_grad), ("wide", "narrow")
    )
    return (
        out_values,
        token_grad,
        norm_summed[0],
        norm_summed[1],
        qkv_summed[:, :local_width],
        qkv_summed[:, local_width : 2 * local_width],
        qkv_summed[:, 2 * local_width :],
        out_summed,
        norm_summed[2],
        norm_summed[3],
        gate_up_summed[:, :local_hidden],
        gate_up_summed[:, local_hidden:],
        down_summed,
    )


def solution(mesh):
    in_specs = (
        P(("wide", "narrow"), None),
        P("wide"),
        P("wide"),
        P(),
        P(),
        P(None, "narrow"),
        P(None, "narrow"),
        P(None, "narrow"),
        P("narrow", None),
        P(),
        P(),
        P(None, "narrow"),
        P(None, "narrow"),
        P("narrow", None),
        P(("wide", "narrow"), None),
    )
    out_specs = (
        P(("wide", "narrow"), None),
        P(("wide", "narrow"), None),
        P(),
        P(),
        P(None, "narrow"),
        P(None, "narrow"),
        P(None, "narrow"),
        P("narrow", None),
        P(),
        P(),
        P(None, "narrow"),
        P(None, "narrow"),
        P("narrow", None),
    )
    return jax.shard_map(
        on_device, mesh=mesh, in_specs=in_specs, out_specs=out_specs, check_vma=False
    )
```

profile of v0, /device:TPU:0, one launch (start us, length us, event | category | flops | bytes accessed | tf_op | source)
XLA Modules:
  0.0 900.9 jit_solution(3977947067159316405)
XLA Ops:
  15.9 10.1 %all-gather.5.cloned.1.call-done = bf16[1024,1024]{1,0:T(8,128)(2,1)} async-done(((bf16[512,1024]{1,0:T(8,128)(2,1)}), bf16[1024,1024]{1,0:T(8,128)(2,1)}) %all-gather.5.cloned.1.call-update) | async-done | bytes 2097168 | tf_op jit(solution)/shard_map/all_gather | solution.py:112
  26.1 5.9 fusion.98
  41.6 3.2 rev.14
  50.5 3.2 rev.13
  56.6 11.1 %fusion.54 = (bf16[1024,512]{1,0:T(8,128)(2,1)}, bf16[1024,512]{1,0:T(8,128)(2,1)S(1)}) fusion(f32[1024,512]{1,0:T(8,128)} %copy.42, f32[512]{0:T(512)S(1)} %get-tuple-element.644, f32[512]{0:T(512)S(1)} %get-tuple-element.643, f32[1024]{0:T(1024)S(1)} %fusion.66, f32[1024,1536]{1,0:T(8,128)} %copy-done.15, f32[1024,512]{1,0:T(8,128)} %copy.40), kind=kLoop, calls=%fused_computation.97 | loop fusion | flops 5767168 | bytes 10493952 | tf_op jit(solution)/shard_map/convert_element_type | solution.py:119
  70.5 44.1 %while.36 = (s32[]{:T(128)}, bf16[2,512,512]{2,1,0:T(8,128)(2,1)}, f32[2,8,512]{2,1,0:T(8,128)S(1)}, s32[2]{0:T(128)S(1)}, s32[2]{0:T(128)S(1)}, /*index=5*/s32[...) while((s32[]{:T(128)}, bf16[2,512,512]{2,1,0:T(8,128)(2,1)}, ...), condition=%wide.region_5.6_spmd, body=%wide.region_2.5_spmd.sunk | while | flops 1111768064 | bytes 56758836 | solution.py:156
  83.0 3.5 fusion.161
  86.5 4.9 fusion.162
  105.0 3.5 fusion.161
  108.5 4.9 fusion.162
  114.5 4.5 fusion.99
  119.1 13.3 %reduce-scatter.5.cloned.1.call-done = f32[512,1024]{1,0:T(8,128)} async-done(((f32[1024,1024]{1,0:T(8,128)}), f32[512,1024]{1,0:T(8,128)}) %reduce-scatter.5.cloned.1.call-update) | async-done | bytes 2097168 | tf_op jit(solution)/shard_map/reduce_scatter | solution.py:158
  137.7 4.9 constant_dynamic-update-slice_fusion.6
  144.9 4.1 all-gather.7.cloned.1.call-done
  149.0 16.4 %fusion.100 = f32[1024,4096]{1,0:T(8,128)} fusion(bf16[1024,1024]{1,0:T(8,128)(2,1)} %all-gather.7.cloned.1.call-done, bf16[1024,4096]{1,0:T(8,128)(2,1)} %constant_dynamic-update-slice_fusion.5), kind=kOutput, calls=%fused_computation.183 | convolution fusion | flops 8589934592 | bytes 27262976 | tf_op jit(solution)/shard_map/dot_general | solution.py:168
  165.5 15.5 %multiply_convert_fusion.2 = (bf16[1024,2048]{1,0:T(8,128)(2,1)S(1)}, bf16[1024,2048]{1,0:T(8,128)(2,1)}, bf16[1024,2048]{1,0:T(8,128)(2,1)}) fusion(f32[1024,4096]{1,0:T(8,128)} %fusion.100, bf16[1024,1024]{1,0:T(8,128)(2,1)} %all-gather.9.cloned.1.call-done, bf16[2048,1024]{1,0:T(8,128)(2,1)} %param.32), kind=kOutput, calls=%fused_computation.59 | convolution fusion | flops 4328521728 | bytes 35651584 | tf_op jit(solution)/shard_map/dot_general | solution.py:13
  182.9 13.9 %fusion.31 = f32[1024,1024]{1,0:T(8,128)} fusion(bf16[1024,4096]{1,0:T(8,128)(2,1)} %constant_dynamic-update-slice_fusion.5, bf16[1024,2048]{1,0:T(8,128)(2,1)} %get-tuple-element.627, bf16[1024,2048]{1,0:T(8,128)(2,1)S(1)} %get-tuple-element.626), kind=kOutput, calls=%fused_computation.63 | convolution fusion | flops 8606711808 | bytes 20971520 | tf_op jit(solution)/shard_map/dot_general | solution.py:13
  196.9 9.3 %convolution_convert_fusion.4 = bf16[1024,1024]{1,0:T(8,128)(2,1)} fusion(bf16[1024,2048]{1,0:T(8,128)(2,1)} %get-tuple-element.628, bf16[2048,1024]{1,0:T(8,128)(2,1)} %param.32), kind=kOutput, calls=%fused_computation.117 | convolution fusion | flops 4296015872 | bytes 10485760 | tf_op jit(solution)/shard_map/dot_general | solution.py:174
  206.3 4.0 reduce-scatter.9.cloned.1.call-done
  210.3 3.7 multiply_reduce_fusion.1
  214.0 10.1 %reduce-scatter.7.cloned.1.call-done = bf16[512,1024]{1,0:T(8,128)(2,1)} async-done(((bf16[1024,1024]{1,0:T(8,128)(2,1)}), bf16[512,1024]{1,0:T(8,128)(2,1)}) %reduce-scatter.7.cloned.1.call-update) | async-done | bytes 1048592 | tf_op jit(solution)/shard_map/reduce_scatter | solution.py:173
  224.0 5.8 fusion.88
  229.9 11.9 %all-gather.11.cloned.1.call-done = bf16[1024,1024]{1,0:T(8,128)(2,1)} async-done(((bf16[512,1024]{1,0:T(8,128)(2,1)}), bf16[1024,1024]{1,0:T(8,128)(2,1)}) %all-gather.11.cloned.1.call-update) | async-done | bytes 2097168 | tf_op jit(solution)/shard_map/all_gather | solution.py:194
  241.8 3.8 convolution_convert_fusion.6
  247.3 94.5 %while.37 = (s32[]{:T(128)}, f32[1024,512]{1,0:T(8,128)}, f32[1024,512]{0,1:T(8,128)}, f32[1024,512]{0,1:T(8,128)}, s32[2]{0:T(128)S(1)}, /*index=5*/s32[2]{0:T(...) while((s32[]{:T(128)}, f32[1024,512]{1,0:T(8,128)}, ...), condition=%wide.region_15.16_spmd.clone, body=%wide.region_13.15_spmd.clone.sunk | while | flops 2736798720 | bytes 236049072 | solution.py:233
  255.4 4.2 fusion.177
  259.6 9.7 %multiply_reduce_fusion.6 = (f32[8,512]{1,0:T(8,128)S(1)}, f32[8,512,1024]{2,1,0:T(8,128)}) fusion(f32[8,512,1024]{2,1,0:T(8,128)S(1)} %fusion.173, f32[8,512]{1,0:T(8,128)S(1)} %dynamic-slice_bitcast_fusion.2, pred[1024]{0:T(1024)(128)(4,1)S(1)} %fusion.175, bf16[512,8,64]{0,2,1:T(8,128)(2,1)S(1)} %bitcast.141, bf16[1024,8,64]{0,2,1:T(8,128)(2,1)} %bitcast.133), kind=kOutput, calls=%fused_computation.27.clone.1 | convolution fusion | flops 553644032 | bytes 35161088 | tf_op jit(solution)/shard_map/while/body/eval_jaxpr/qhd,khd->hqk/dot_general | solution.py:208
  269.3 10.4 %multiply_convert_fusion.5 = bf16[8,512,1024]{2,1,0:T(8,128)(2,1)} fusion(f32[8,512,1024]{2,1,0:T(8,128)} %get-tuple-element.783, f32[8,512,1024]{2,1,0:T(8,128)S(1)} %fusion.173, f32[8,512]{1,0:T(8,128)S(1)} %get-tuple-element.784, f32[8,512]{1,0:T(8,128)S(1)} %dynamic-slice_bitcast_fusion.2, pred[1024]{0:T(1024)(128)(4,1)S(1)} %fusion.175), kind=kLoop, calls=%fused_computation.26.clone.1 | loop fusion | flops 20971520 | bytes 41976832 | tf_op jit(solution)/shard_map/while/body/eval_jaxpr/convert_element_type | solution.py:212
  279.7 7.2 fusion.176
  302.5 4.2 fusion.177
  306.8 9.7 %multiply_reduce_fusion.6 = (f32[8,512]{1,0:T(8,128)S(1)}, f32[8,512,1024]{2,1,0:T(8,128)}) fusion(f32[8,512,1024]{2,1,0:T(8,128)S(1)} %fusion.173, f32[8,512]{1,0:T(8,128)S(1)} %dynamic-slice_bitcast_fusion.2, pred[1024]{0:T(1024)(128)(4,1)S(1)} %fusion.175, bf16[512,8,64]{0,2,1:T(8,128)(2,1)S(1)} %bitcast.141, bf16[1024,8,64]{0,2,1:T(8,128)(2,1)} %bitcast.133), kind=kOutput, calls=%fused_computation.27.clone.1 | convolution fusion | flops 553644032 | bytes 35161088 | tf_op jit(solution)/shard_map/while/body/eval_jaxpr/qhd,khd->hqk/dot_general | solution.py:208
  316.5 10.4 %multiply_convert_fusion.5 = bf16[8,512,1024]{2,1,0:T(8,128)(2,1)} fusion(f32[8,512,1024]{2,1,0:T(8,128)} %get-tuple-element.783, f32[8,512,1024]{2,1,0:T(8,128)S(1)} %fusion.173, f32[8,512]{1,0:T(8,128)S(1)} %get-tuple-element.784, f32[8,512]{1,0:T(8,128)S(1)} %dynamic-slice_bitcast_fusion.2, pred[1024]{0:T(1024)(128)(4,1)S(1)} %fusion.175), kind=kLoop, calls=%fused_computation.26.clone.1 | loop fusion | flops 20971520 | bytes 41976832 | tf_op jit(solution)/shard_map/while/body/eval_jaxpr/convert_element_type | solution.py:212
  326.9 7.2 fusion.176
  346.0 9.4 %fusion.61 = (f32[1024,512]{1,0:T(8,128)}, f32[1024,512]{1,0:T(8,128)S(1)}) fusion(f32[1024,512]{1,0:T(8,128)} %get-tuple-element.477, f32[512]{0:T(512)S(1)} %copy-done.45, f32[512]{0:T(512)S(1)} %copy-done.43, f32[1024]{0:T(1024)S(1)} %copy-done.34, f32[1024,512]{1,0:T(8,128)} %copy.54), kind=kLoop, calls=%fused_computation.104 | loop fusion | flops 2621440 | bytes 8396800 | tf_op jit(solution)/shard_map/mul | solution.py:69
  358.3 3.2 rev.15
  366.1 3.2 rev.16
  369.3 3.0 copy.57
  372.3 9.1 %fusion.56 = (bf16[1024,512]{1,0:T(8,128)(2,1)S(1)}, bf16[1024,512]{1,0:T(8,128)(2,1)S(1)}) fusion(f32[1024,512]{1,0:T(8,128)} %copy.53, f32[1024,512]{1,0:T(8,128)} %get-tuple-element.477, f32[512]{0:T(512)S(1)} %copy-done.43, f32[1024]{0:T(1024)S(1)} %copy-done.34, f32[1024,512]{1,0:T(8,128)} %copy.57, f32[1024,512]{1,0:T(8,128)S(1)} %copy-done.14), kind=kLoop, calls=%fused_computation.99 | loop fusion | flops 4194304 | bytes 10491904 | tf_op jit(solution)/shard_map/convert
  382.8 4.6 convolution_convert_fusion.3
  389.0 8.7 convolution_convert_fusion.2
  397.7 11.5 %convolution_convert_fusion = bf16[1024,4096]{1,0:T(8,128)(2,1)} fusion(bf16[1024,1024]{1,0:T(8,128)(2,1)S(1)} %copy-done.51, bf16[1024,2048]{1,0:T(8,128)(2,1)S(1)} %copy-done.56, bf16[1024,2048]{1,0:T(8,128)(2,1)S(1)} %copy-done.55), kind=kOutput, calls=%fused_computation.62 | convolution fusion | flops 8610906112 | bytes 18874368 | tf_op jit(solution)/shard_map/dot_general | solution.py:19
  411.6 5.5 convolution_convert_fusion.1
  420.6 44.3 %all-reduce = (f32[1024]{0:T(1024)}, f32[1024]{0:T(1024)}, f32[1024]{0:T(1024)}, f32[1024]{0:T(1024)}) all-reduce(f32[1024]{0:T(1024)S(1)} %get-tuple-element.559, f32[1024]{0:T(1024)S(1)} %get-tuple-element.563, f32[1024]{0:T(1024)S(1)} %copy-done.46, f32[1024]{0:T(1024)S(1)} %copy-done.47), channel_id=1, replica_groups=mesh['wide'=16,'narrow'=2] {'wide','narrow'}, use_global_device_ids=true, to_apply=%region_20.21 | all-reduce | flops 4096 | bytes 32768 | tf_op jit(solution)/shard_map/psum | solution.py:258
  465.0 3.7 fusion.47
  468.7 401.7 %all-reduce.4.cloned.1.call-done = (bf16[1024,1536]{1,0:T(8,128)(2,1)}, bf16[512,1024]{1,0:T(8,128)(2,1)}, bf16[1024,4096]{1,0:T(8,128)(2,1)}, bf16[2048,1024]{1,0:T(8,128)(2,1)}) async-done(((bf16[1024,1536]{1,0:T(8,128)(2,1)}, bf16[512,1024]{1,0:T(8,128)(2,1)}, bf16[1024,4096]{1,0:T(8,128)(2,1)}, bf16[2048,1024]{1,0:T(8,128)(2,1)}), (bf16[1024,1536]{1,0:T(8,128)(2,1)}, bf16[512,1024]{1,0:T(8,128)(2,1)}, ...) | async-done | bytes 16777232 | tf_op jit(solution)/shard_map/psum | solution.py:253
  873.3 3.4 fusion.94
  877.7 4.4 convert_element_type.152
  882.1 11.8 %fusion.92 = (f32[1024,2048]{1,0:T(8,128)}, f32[1024,2048]{1,0:T(8,128)}) fusion(bf16[1024,4096]{1,0:T(8,128)(2,1)} %get-tuple-element.610), kind=kLoop, calls=%fused_computation.175 | loop fusion | bytes 33554432 | tf_op jit(solution)/shard_map/slice | solution.py:273
  (236 shorter events, 111.9 us)
Async XLA Ops:
  7.2 107.4 %copy-start = (bf16[512,1024]{1,0:T(8,128)(2,1)S(1)}, bf16[512,1024]{1,0:T(8,128)(2,1)}, u32[]{:S(2)}) copy-start(bf16[512,1024]{1,0:T(8,128)(2,1)} %param.27) | copy-start | bytes 3145732
  7.2 4.0 copy-start.11
  7.2 4.0 copy-start.38
  7.2 4.0 copy-start.48
  7.2 18.8 %all-gather.5.cloned.1.call-start = ((), (), s32[]{:S(2)}) async-start(), calls=%async_computation.4 | async-start | bytes 3145728 | tf_op jit(solution)/shard_map/all_gather | solution.py:112
  8.9 3.8 copy-start.53
  8.9 4.0 copy-start.22
  12.6 119.8 %reduce-scatter.5.cloned.1.call-start = ((), (), s32[]{:S(2)}) async-start(), calls=%async_computation.5 | async-start | bytes 6291456 | tf_op jit(solution)/shard_map/reduce_scatter | solution.py:158
  12.8 43.7 %copy-start.42 = (f32[512]{0:T(512)}, f32[512]{0:T(512)S(1)}, u32[]{:S(2)}) copy-start(f32[512]{0:T(512)S(1)} %get-tuple-element.643) | copy-start | bytes 6148
  12.8 43.7 %copy-start.44 = (f32[512]{0:T(512)}, f32[512]{0:T(512)S(1)}, u32[]{:S(2)}) copy-start(f32[512]{0:T(512)S(1)} %get-tuple-element.644) | copy-start | bytes 6148
  15.9 40.6 %copy-start.33 = (f32[1024]{0:T(1024)}, f32[1024]{0:T(1024)S(1)}, u32[]{:S(2)}) copy-start(f32[1024]{0:T(1024)S(1)} %fusion.66) | copy-start | bytes 12292
  32.0 2.7 copy-start.15
  67.6 2.8 copy-start.32
  119.0 13.4 %copy-start.12 = (bf16[512,1024]{1,0:T(8,128)(2,1)S(1)}, bf16[512,1024]{1,0:T(8,128)(2,1)}, u32[]{:S(2)}) copy-start(bf16[512,1024]{1,0:T(8,128)(2,1)} %param.19) | copy-start | bytes 3145732
  119.0 30.0 %all-gather.7.cloned.1.call-start = ((), (), s32[]{:S(2)}) async-start(), calls=%async_computation.6 | async-start | bytes 3145728 | tf_op jit(solution)/shard_map/all_gather | solution.py:166
  137.0 28.5 %all-gather.9.cloned.1.call-start = ((), (), s32[]{:S(2)}) async-start(), calls=%async_computation.8 | async-start | bytes 3145728 | tf_op jit(solution)/shard_map/all_gather | solution.py:179
  137.6 72.7 %reduce-scatter.9.cloned.1.call-start = ((), (), s32[]{:S(2)}) async-start(), calls=%async_computation.9 | async-start | bytes 6291456 | tf_op jit(solution)/shard_map/reduce_scatter | solution.py:186
  137.7 5.0 copy-start.19
  196.9 27.1 %reduce-scatter.7.cloned.1.call-start = ((), (), s32[]{:S(2)}) async-start(), calls=%async_computation.7 | async-start | bytes 3145728 | tf_op jit(solution)/shard_map/reduce_scatter | solution.py:173
  206.2 17.8 %copy-start.18 = (bf16[512,1024]{1,0:T(8,128)(2,1)S(1)}, bf16[512,1024]{1,0:T(8,128)(2,1)}, u32[]{:S(2)}) copy-start(bf16[512,1024]{1,0:T(8,128)(2,1)} %param.33) | copy-start | bytes 3145732
  206.2 35.6 %all-gather.11.cloned.1.call-start = ((), (), s32[]{:S(2)}) async-start(), calls=%async_computation.10 | async-start | bytes 3145728 | tf_op jit(solution)/shard_map/all_gather | solution.py:194
  229.8 187.3 %reduce-scatter.11.cloned.1.call-start = ((), (), s32[]{:S(2)}) async-start(), calls=%async_computation.11 | async-start | bytes 3145728 | tf_op jit(solution)/shard_map/reduce_scatter | solution.py:241
  279.7 7.2 copy-start.2
  286.9 2.2 copy-start.5
  286.9 2.9 copy-start.7
  289.7 3.5 copy-start.4
  326.9 7.2 copy-start.2
  334.0 2.2 copy-start.5
  334.0 2.9 copy-start.7
  336.9 3.5 copy-start.4
  341.8 2.2 copy-start.9
  369.3 3.0 copy-start.14
  372.3 10.4 %copy-start.31 = (bf16[1024,1536]{1,0:T(8,128)(2,1)S(1)}, bf16[1024,1536]{1,0:T(8,128)(2,1)}, u32[]{:S(2)}) copy-start(bf16[1024,1536]{1,0:T(8,128)(2,1)} %copy-done.30) | copy-start | bytes 9437188
  387.4 482.9 %all-reduce.4.cloned.1.call-start = ((), (), s32[]{:S(2)}) async-start(), calls=%async_computation.12 | async-start | bytes 33554432 | tf_op jit(solution)/shard_map/psum | solution.py:253
  389.0 8.8 copy-start.51
  389.0 8.8 copy-start.55
  389.0 8.8 copy-start.56
  397.7 11.5 %copy-start.21 = (bf16[1024,1024]{1,0:T(8,128)(2,1)S(1)}, bf16[1024,1024]{1,0:T(8,128)(2,1)}, u32[]{:S(2)}) copy-start(bf16[1024,1024]{1,0:T(8,128)(2,1)} %all-gather.11.cloned.1.call-done) | copy-start | bytes 6291460
  397.7 11.5 %copy-start.25 = (bf16[2,512,512]{2,1,0:T(8,128)(2,1)S(1)}, bf16[2,512,512]{2,1,0:T(8,128)(2,1)}, u32[]{:S(2)}) copy-start(bf16[2,512,512]{2,1,0:T(8,128)(2,1)} %get-tuple-element.475) | copy-start | bytes 3145732
  409.3 2.3 copy-start.27
  409.3 2.3 copy-start.29
  409.3 2.3 copy-start.50
  417.1 3.5 copy-start.46
  417.1 3.5 copy-start.47
  418.3 46.7 %copy-start.20 = (bf16[512,1024]{1,0:T(8,128)(2,1)S(1)}, bf16[512,1024]{1,0:T(8,128)(2,1)}, u32[]{:S(2)}) copy-start(bf16[512,1024]{1,0:T(8,128)(2,1)} %reduce-scatter.11.cloned.1.call-done) | copy-start | bytes 3145732
  870.3 2.9 copy-start.16
  873.3 4.4 copy-start.17
  882.1 11.8 %copy-start.1 = (bf16[512,1024]{1,0:T(8,128)(2,1)S(1)}, bf16[512,1024]{1,0:T(8,128)(2,1)}, u32[]{:S(2)}) copy-start(bf16[512,1024]{1,0:T(8,128)(2,1)} %param.27) | copy-start | bytes 3145732
  (25 other events, 37.1 us)
Sparse Core Ops, SparseCore 0:
  12.7 13.2 all-gather.4
  119.2 13.2 reduce-scatter.4
  137.1 11.8 all-gather.6
  150.4 11.7 all-gather.8
  197.0 13.2 reduce-scatter.8
  212.9 11.0 reduce-scatter.6
  229.9 11.8 all-gather.10
  387.5 10.9 reduce-scatter.10
  417.2 453.0 all-reduce.3
where the time goes:
time: 906 us; the launch traced here: 901 us
  waiting for transfers between devices  456 us (50%)
  matrix products  167 us (18%)
  local copies, waits for them, and re-layouts  108 us (12%)
  other arithmetic  98.1 us (11%)
  blocking collectives  44.3 us (5%)
  between operations  14.8 us (2%)
  loops' own time  12.2 us (1%)
    psum x1, waiting for transfers between devices, on_device(): lax.psum(grad_qkv_w.astype(jnp.bfloat16), 'wide').astype(jnp.float32)  402 us
    psum x1, blocking collectives, on_device(): lax.psum((gain_one_grad, shift_one_grad, gain_two_grad, shift_two_grad),...  44.3 us
    dot_general x4, matrix products, times_transpose(): lax.dot_general(left, right, (((1,), (1,)), ((), ())), preferred_element_...  37.9 us
    dot_general x4, matrix products, transpose_times(): lax.dot_general(left, right, (((0,), (0,)), ((), ())), preferred_element_...  28 us
    convert_element_type x2, other arithmetic, attend_backward(): grad_scores = (attention_probs * (grad_probs - centre)).astype(jnp.bfloat16)  20.8 us
    dot_general x2, matrix products, attend_backward(): jnp.einsum('qhd,khd->hqk', grad_rows, value_pair, preferred_element_type=...  19.4 us
    unnamed x103, local copies, waits for them, and re-layouts  19.3 us
  transfers between devices with their start and end apart: 9, of which 7 were waited for; matrix products, arithmetic and copies ran while one was open for 8% of the time, Pallas kernels for 0%

commit v1 on v0

--- a/solution.py
+++ b/solution.py
@@ -250,7 +250,9 @@
     )
     token_grad = grad_resid + grad_in_one
     qkv_summed, out_summed, gate_up_summed, down_summed = (
-        lax.psum(grad_qkv_w.astype(jnp.bfloat16), "wide").astype(jnp.float32),
+        jnp.sum(lax.all_gather(grad_qkv_w.astype(jnp.bfloat16), "wide"), axis=0).astype(
+            jnp.float32
+        ),
         lax.psum(grad_out_w.astype(jnp.bfloat16), "wide").astype(jnp.float32),
         lax.psum(grad_gate_up_w.astype(jnp.bfloat16), "wide").astype(jnp.float32),
         lax.psum(grad_down_w.astype(jnp.bfloat16), "wide").astype(jnp.float32),

time: 906 us -> 1350 us (1.49)
  waiting for transfers between devices: 456 us -> 866 us
  other arithmetic: 98.1 us -> 125 us
    all_gather x0 -> x1, waiting for transfers between devices: none -> 488 us  [on_device(): lax.all_gather(grad_qkv_w.astype(jnp.bfloat16), 'wide')]
    psum x1, waiting for transfers between devices: 402 us -> 325 us  [on_device(): lax.psum(grad_out_w.astype(jnp.bfloat16), 'wide').astype(jnp.float32)]
    reduce_sum x0 -> x1, other arithmetic: none -> 18.7 us  [on_device(): jnp.sum(lax.all_gather(grad_qkv_w.astype(jnp.bfloat16), 'wide'), axis=0)]
  transfers between devices with their start and end apart: 9 -> 10, of which waited for: 7 -> 8; matrix products, arithmetic and copies ran while one was open for 8% -> 7% of each run, Pallas kernels for 0% -> 0%
where the time goes in v1:
time: 1350 us; the launch traced here: 1340 us
  waiting for transfers between devices  866 us (64%)
  matrix products  168 us (12%)
  other arithmetic  125 us (9%)
  local copies, waits for them, and re-layouts  109 us (8%)
  blocking collectives  44.2 us (3%)
  between operations  15.1 us (1%)
    all_gather x1, waiting for transfers between devices, on_device(): lax.all_gather(grad_qkv_w.astype(jnp.bfloat16), 'wide')  488 us
    psum x1, waiting for transfers between devices, on_device(): lax.psum(grad_out_w.astype(jnp.bfloat16), 'wide').astype(jnp.float32)  325 us
    psum x1, blocking collectives, on_device(): lax.psum((gain_one_grad, shift_one_grad, gain_two_grad, shift_two_grad),...  44.2 us
    dot_general x4, matrix products, times_transpose(): lax.dot_general(left, right, (((1,), (1,)), ((), ())), preferred_element_...  37.9 us
    dot_general x4, matrix products, transpose_times(): lax.dot_general(left, right, (((0,), (0,)), ((), ())), preferred_element_...  30.4 us
  transfers between devices with their start and end apart: 10, of which 8 were waited for; matrix products, arithmetic and copies ran while one was open for 7% of the time, Pallas kernels for 0%

profile of v1, /device:TPU:0, one launch (start us, length us, event | category | flops | bytes accessed | tf_op | source)
XLA Modules:
  0.0 1340.3 jit_solution(10902470049694580814)
XLA Ops:
  16.0 10.1 all-gather.7.cloned.1.call-done
  26.1 5.9 fusion.98
  51.2 10.9 fusion.54
  65.9 44.1 %while.36 = (s32[]{:T(128)}, bf16[2,512,512]{2,1,0:T(8,128)(2,1)}, f32[2,8,512]{2,1,0:T(8,128)}, s32[2]{0:T(128)S(1)}, s32[2]{0:T(128)S(1)}, /*index=5*/s32[2]{0...) while((s32[]{:T(128)}, bf16[2,512,512]{2,1,0:T(8,128)(2,1)}, ...), condition=%wide.region_5.6_spmd, body=%wide.region_2.5_spmd.sunk | while | flops 1111768064 | bytes 60953168 | solution.py:156
  78.4 3.5 fusion.161
  82.0 4.3 fusion.162
  100.5 3.5 fusion.161
  104.0 4.3 fusion.162
  110.0 4.5 fusion.99
  114.8 13.1 reduce-scatter.5.cloned.1.call-done
  133.4 4.9 constant_dynamic-update-slice_fusion.6
  140.7 4.1 all-gather.9.cloned.1.call-done
  144.8 16.0 %fusion.100 = f32[1024,4096]{1,0:T(8,128)} fusion(bf16[1024,1024]{1,0:T(8,128)(2,1)} %all-gather.9.cloned.1.call-done, bf16[1024,4096]{1,0:T(8,128)(2,1)} %constant_dynamic-update-slice_fusion.5), kind=kOutput, calls=%fused_computation.183 | convolution fusion | flops 8589934592 | bytes 27262976 | tf_op jit(solution)/shard_map/dot_general | solution.py:168
  160.8 15.5 %multiply_convert_fusion.2 = (bf16[1024,2048]{1,0:T(8,128)(2,1)S(1)}, bf16[1024,2048]{1,0:T(8,128)(2,1)}, bf16[1024,2048]{1,0:T(8,128)(2,1)}) fusion(f32[1024,4096]{1,0:T(8,128)} %fusion.100, bf16[1024,1024]{1,0:T(8,128)(2,1)} %all-gather.11.cloned.1.call-done, bf16[2048,1024]{1,0:T(8,128)(2,1)} %param.32), kind=kOutput, calls=%fused_computation.59 | convolution fusion | flops 4328521728 | bytes 35651584 | tf_op jit(solution)/shard_map/dot_general | solution.py:13
  178.3 13.9 %fusion.31 = f32[1024,1024]{1,0:T(8,128)} fusion(bf16[1024,4096]{1,0:T(8,128)(2,1)} %constant_dynamic-update-slice_fusion.5, bf16[1024,2048]{1,0:T(8,128)(2,1)} %get-tuple-element.626, bf16[1024,2048]{1,0:T(8,128)(2,1)S(1)} %get-tuple-element.625), kind=kOutput, calls=%fused_computation.63 | convolution fusion | flops 8606711808 | bytes 20971520 | tf_op jit(solution)/shard_map/dot_general | solution.py:13
  192.7 9.3 convolution_convert_fusion.4
  202.0 3.6 reduce-scatter.9.cloned.1.call-done
  205.6 3.7 multiply_reduce_fusion.1
  209.3 10.1 reduce-scatter.7.cloned.1.call-done
  219.3 6.1 fusion.88
  225.5 11.9 all-gather.13.cloned.1.call-done
  237.5 3.8 convolution_convert_fusion.6
  242.9 102.3 %while.37 = (s32[]{:T(128)}, f32[1024,512]{1,0:T(8,128)}, f32[1024,512]{0,1:T(8,128)}, f32[1024,512]{0,1:T(8,128)}, s32[2]{0:T(128)S(1)}, /*index=5*/s32[2]{0:T(...) while((s32[]{:T(128)}, f32[1024,512]{1,0:T(8,128)}, ...), condition=%wide.region_15.16_spmd.clone, body=%wide.region_13.15_spmd.clone.sunk | while | flops 2736798720 | bytes 219271792 | solution.py:233
  251.5 4.2 fusion.177
  255.7 9.7 multiply_reduce_fusion.6
  265.4 10.4 multiply_convert_fusion.5
  275.8 7.2 fusion.176
  301.8 4.2 fusion.177
  306.1 9.7 multiply_reduce_fusion.6
  315.7 10.4 multiply_convert_fusion.5
  326.1 7.2 fusion.176
  335.5 4.6 bitcast_add_fusion.3
  349.2 9.4 fusion.61
  361.5 3.2 rev.15
  369.3 3.2 rev.16
  375.5 9.1 fusion.56
  385.9 4.6 convolution_convert_fusion.3
  390.7 9.5 convolution_convert_fusion.2
  400.2 11.7 convolution_convert_fusion
  415.7 6.9 convolution_convert_fusion.1
  426.1 44.2 %all-reduce = (f32[1024]{0:T(1024)}, f32[1024]{0:T(1024)}, f32[1024]{0:T(1024)}, f32[1024]{0:T(1024)}) all-reduce(f32[1024]{0:T(1024)S(1)} %get-tuple-element.559, f32[1024]{0:T(1024)S(1)} %get-tuple-element.563, f32[1024]{0:T(1024)S(1)} %copy-done.42, f32[1024]{0:T(1024)S(1)} %copy-done.43), channel_id=1, replica_groups=mesh['wide'=16,'narrow'=2] {'wide','narrow'}, use_global_device_ids=true, to_apply=%region_20.21 | all-reduce | flops 4096 | bytes 32768 | tf_op jit(solution)/shard_map/psum | solution.py:260
  470.3 3.3 fusion.47
  473.6 325.2 %all-reduce.4.cloned.1.call-done = (bf16[512,1024]{1,0:T(8,128)(2,1)}, bf16[1024,4096]{1,0:T(8,128)(2,1)}, bf16[2048,1024]{1,0:T(8,128)(2,1)}) async-done(((bf16[512,1024]{1,0:T(8,128)(2,1)}, bf16[1024,4096]{1,0:T(8,128)(2,1)}, bf16[2048,1024]{1,0:T(8,128)(2,1)}), (bf16[512,1024]{1,0:T(8,128)(2,1)}, bf16[1024,4096]{1,0:T(8,128)(2,1)}, bf16[2048,1024]{1,0:T(8,128)(2,1)})) %all-reduce.4.cloned.1.call-update) | async-done | bytes 13631504 | tf_op jit(solution)/shard_map/psum | solution.py:256
  801.6 6.6 convert_element_type.154
  808.3 13.4 fusion.92
  821.6 487.6 %all-gather.15.cloned.1.call-done = bf16[16384,1536]{1,0:T(8,128)(2,1)} async-done(((bf16[1024,1536]{1,0:T(8,128)(2,1)}), bf16[16384,1536]{1,0:T(8,128)(2,1)}) %all-gather.15.cloned.1.call-update) | async-done | bytes 50331664 | tf_op jit(solution)/shard_map/all_gather | solution.py:253
  1309.3 18.7 %reduce_sum.160 = bf16[1024,1536]{1,0:T(8,128)(2,1)} reduce(bf16[16,1024,1536]{2,1,0:T(8,128)(2,1)} %bitcast.145, bf16[]{:T(256)} %constant.365.clone.1), dimensions={0}, to_apply=%region_23.24 | reduce | flops 23592960 | bytes 53477376 | tf_op jit(solution)/shard_map/reduce_sum | solution.py:253
  1328.0 5.0 fusion.94
  (226 shorter events, 120.8 us)
Async XLA Ops:
  7.2 102.8 %copy-start = (bf16[512,1024]{1,0:T(8,128)(2,1)S(1)}, bf16[512,1024]{1,0:T(8,128)(2,1)}, u32[]{:S(2)}) copy-start(bf16[512,1024]{1,0:T(8,128)(2,1)} %param.27) | copy-start | bytes 3145732
  7.2 4.0 copy-start.10
  7.2 4.0 copy-start.34
  7.2 4.0 copy-start.44
  7.2 18.9 %all-gather.7.cloned.1.call-start = ((), (), s32[]{:S(2)}) async-start(), calls=%async_computation.4 | async-start | bytes 3145728 | tf_op jit(solution)/shard_map/all_gather | solution.py:112
  8.9 1.8 copy-start.31
  8.9 3.9 copy-start.47
  8.9 4.0 copy-start.18
  12.7 115.2 %reduce-scatter.5.cloned.1.call-start = ((), (), s32[]{:S(2)}) async-start(), calls=%async_computation.5 | async-start | bytes 6291456 | tf_op jit(solution)/shard_map/reduce_scatter | solution.py:158
  12.9 38.3 %copy-start.38 = (f32[512]{0:T(512)}, f32[512]{0:T(512)S(1)}, u32[]{:S(2)}) copy-start(f32[512]{0:T(512)S(1)} %get-tuple-element.642) | copy-start | bytes 6148
  12.9 38.3 %copy-start.40 = (f32[512]{0:T(512)}, f32[512]{0:T(512)S(1)}, u32[]{:S(2)}) copy-start(f32[512]{0:T(512)S(1)} %get-tuple-element.643) | copy-start | bytes 6148
  16.0 35.2 %copy-start.29 = (f32[1024]{0:T(1024)}, f32[1024]{0:T(1024)S(1)}, u32[]{:S(2)}) copy-start(f32[1024]{0:T(1024)S(1)} %fusion.66) | copy-start | bytes 12292
  32.0 2.7 copy-start.13
  48.2 3.0 copy-start.15
  62.1 3.8 copy-start.28
  78.4 3.6 copy-start.9
  100.5 3.6 copy-start.9
  114.5 30.3 %all-gather.9.cloned.1.call-start = ((), (), s32[]{:S(2)}) async-start(), calls=%async_computation.6 | async-start | bytes 3145728 | tf_op jit(solution)/shard_map/all_gather | solution.py:166
  132.8 28.0 %all-gather.11.cloned.1.call-start = ((), (), s32[]{:S(2)}) async-start(), calls=%async_computation.8 | async-start | bytes 3145728 | tf_op jit(solution)/shard_map/all_gather | solution.py:179
  133.3 72.2 %reduce-scatter.9.cloned.1.call-start = ((), (), s32[]{:S(2)}) async-start(), calls=%async_computation.9 | async-start | bytes 6291456 | tf_op jit(solution)/shard_map/reduce_scatter | solution.py:186
  133.4 5.0 copy-start.16
  176.3 2.0 copy-start.48
  192.2 27.1 %reduce-scatter.7.cloned.1.call-start = ((), (), s32[]{:S(2)}) async-start(), calls=%async_computation.7 | async-start | bytes 3145728 | tf_op jit(solution)/shard_map/reduce_scatter | solution.py:173
  202.0 35.5 %all-gather.13.cloned.1.call-start = ((), (), s32[]{:S(2)}) async-start(), calls=%async_computation.10 | async-start | bytes 3145728 | tf_op jit(solution)/shard_map/all_gather | solution.py:194
  225.5 197.2 %reduce-scatter.11.cloned.1.call-start = ((), (), s32[]{:S(2)}) async-start(), calls=%async_computation.11 | async-start | bytes 3145728 | tf_op jit(solution)/shard_map/reduce_scatter | solution.py:241
  275.8 7.2 copy-start.2
  283.0 2.2 copy-start.5
  285.2 4.5 copy-start.4
  326.1 7.2 copy-start.2
  333.3 2.2 copy-start.5
  335.5 5.9 copy-start.4
  345.2 2.2 copy-start.7
  347.4 1.8 copy-start.30
  347.4 1.8 copy-start.39
  347.4 1.8 copy-start.41
  372.5 3.0 copy-start.12
  375.5 10.4 copy-start.27
  390.6 9.6 copy-start.46
  390.6 408.3 %all-reduce.4.cloned.1.call-start = ((), (), s32[]{:S(2)}) async-start(), calls=%async_computation.13 | async-start | bytes 27262976 | tf_op jit(solution)/shard_map/psum | solution.py:256
  390.6 9.6 copy-start.49
  390.6 9.6 copy-start.50
  400.2 11.7 copy-start.17
  400.2 11.7 copy-start.21
  414.2 895.1 %all-gather.15.cloned.1.call-start = ((), (), s32[]{:S(2)}) async-start(), calls=%async_computation.12 | async-start | bytes 53477376 | tf_op jit(solution)/shard_map/all_gather | solution.py:253
  422.6 3.5 copy-start.42
  422.6 3.5 copy-start.43
  422.7 47.7 %copy-start.14 = (f32[512,1024]{1,0:T(8,128)S(1)}, f32[512,1024]{1,0:T(8,128)}, u32[]{:S(2)}) copy-start(f32[512,1024]{1,0:T(8,128)} %get-tuple-element.612) | copy-start | bytes 6291460
  1328.0 5.0 copy-start.1
  (19 other events, 24.5 us)
Sparse Core Ops, SparseCore 0:
  12.8 13.2 all-gather.6
  114.7 13.2 reduce-scatter.4
  132.9 11.8 all-gather.8
  146.2 11.7 all-gather.10
  192.3 13.2 reduce-scatter.8
  208.3 11.0 reduce-scatter.6
  225.6 11.8 all-gather.12
  390.7 10.9 reduce-scatter.10
  414.3 384.4 all-reduce.3
  801.5 507.7 all-gather.14
